TPU v7x, 32 devices: a whole 2x2x4 slice. The times are simulated.
32 devices in a mesh: ens: 4 (over x, core), lat: 8 (over z, y).
Axes of the slice: x: 2, y: 2, z: 4, core: 2. Of those that a mesh axis runs over, the one named last changes fastest.
Arguments:
- fields: bfloat16 [8, 24, 48, 1440], P('ens', None, 'lat'), may hold values from -6 to 6
- depth_kernel: float32 [24, 7, 7], replicated, may hold values from -0.875 to 0.875
- mix_weight: bfloat16 [24, 24], replicated, may hold values from -1.25 to 1.25
- legendre: bfloat16 [48, 160, 160], P('lat'), may hold values from -1.25 to 1.25
- truth: bfloat16 [24, 2, 160, 160], replicated, may hold values from -6 to 6
- degree_order: int32 [160], replicated, may hold values from 0 to 159, each once
Outputs:
- grad_fields: bfloat16 [8, 24, 48, 1440], P('ens', None, 'lat')
- score_grad: float32 [8, 24, 2, 160, 160], P('ens', None, None, None, 'lat')
Inputs may be any that keep to these rules, and one draw needn't show every extreme that they name: `degree_order`: each degree appears once.
All inputs are finite; a program needn't handle non-finite values.
Results may differ from a plain program's by a relative error of at most 0.02.
Values may be sent and summed in bfloat16 or wider, within the bound.
No kernel may reach another device: no remote copies, remote signals or barrier semaphores. Data moves between devices by JAX's collectives and lax.ppermute only.
A program may use at most 128 MiB of HBM per device.

v0:
```python
import functools
import math

import jax
import jax.numpy as jnp
import numpy as np
from jax import lax
from jax.experimental import pallas as pl
from jax.experimental.pallas import tpu as pltpu
from jax.sharding import PartitionSpec as P


smooth_width = 0.5
TILE = 16
F32 = jnp.float32
BF16 = jnp.bfloat16


def up(value, step):
    return -(-value // step) * step


def wave_table(nlon, orders, span):
    columns = np.arange(nlon, dtype=np.int64)
    number = np.arange(orders, dtype=np.int64)
    angles = (columns[:, None] * number[None, :] % nlon) * (2.0 * math.pi / nlon)
    table = np.zeros((nlon, 2, span), np.float32)
    for part, values in enumerate((np.cos(angles), -np.sin(angles))):
        table[:, part, :orders] = values / math.sqrt(nlon)
    return table.reshape(nlon, 2 * span).astype(jnp.bfloat16)


def partners(inner, outer):
    count = lax.axis_size("lat")
    near = [(i, i ^ 1) for i in range(count)]
    far = [(i, min(max(i + (1 if i % 2 else -1), 0), count - 1)) for i in range(count)]
    one = lax.ppermute(inner, "lat", near)
    other = lax.ppermute(outer, "lat", far)
    return one, other


def place():
    at, count = lax.axis_index("lat"), lax.axis_size("lat")
    return jnp.stack([at % 2, (at > 0) & (at < count - 1)]).astype(jnp.int32)


def fill_row(padded, row, value, half):
    depth, nlon = value.shape
    wide = padded.shape[-1]
    base = nlon // 128 * 128
    tail = [value[:, base:], value[:, :half]]
    if wide > nlon + 2 * half:
        tail.append(jnp.zeros((depth, wide - nlon - 2 * half), value.dtype))
    tail.append(value[:, nlon - half :])
    padded[row, :, :base] = value[:, :base].astype(padded.dtype)
    padded[row, :, base:] = jnp.concatenate(tail, axis=-1).astype(padded.dtype)


def tap_sum(padded, taps, c0, lines, size):
    wide = padded.shape[-1]
    total = None
    for q in range(size):
        part = None
        for row, p in lines:
            weight = jnp.tile(taps[p * size + q, pl.ds(c0, TILE), :], (1, wide // 128))
            term = weight * padded[row, pl.ds(c0, TILE), :]
            part = term if part is None else part + term
        part = part.astype(F32)
        shift = (size // 2 - q) % wide
        if shift:
            part = pltpu.roll(part, shift, 1)
        total = part if total is None else total + part
    return total


def spread_taps(kernel, taps, flip):
    size, _, chans = kernel.shape
    for p in range(size):
        plane = kernel[p].T
        for q in range(size):
            at = p * size + q
            at = size * size - 1 - at if flip else at
            value = jnp.broadcast_to(plane[:, q : q + 1], (chans, 128))
            value = jnp.concatenate([value] * (taps.shape[1] // chans), axis=0)
            taps[at] = value.astype(taps.dtype)


def joined(block, row):
    return jnp.concatenate([block[b, row].astype(F32) for b in range(block.shape[0])], axis=0)


def gelu_pair(x):
    scale = math.sqrt(2.0 / math.pi)
    square = x * x
    t = jnp.tanh(scale * x * (1.0 + 0.044715 * square))
    half = 0.5 * (1.0 + t)
    slope = half + 0.5 * x * (1.0 - t * t) * (scale * (1.0 + 3 * 0.044715 * square))
    return x * half, slope


def prepare_kernel(own, kernel, weight, pick, partial, mixer, padded, taps):
    members, rows, chans, nlon = own.shape
    depth = members * chans
    size = kernel.shape[0]
    half = size // 2
    spread_taps(kernel, taps, False)
    for row in range(rows):
        fill_row(padded, row, joined(own, row), half)

    @pl.loop(0, depth // TILE)
    def _(ct):
        c0 = pl.multiple_of(ct * TILE, TILE)
        for i in range(rows):
            lines = [(i + p - half, p) for p in range(size) if 0 <= i + p - half < rows]
            total = tap_sum(padded, taps, c0, lines, size)
            total = total + padded[i, pl.ds(c0, TILE), :].astype(F32)
            partial[i, pl.ds(c0, TILE), :] = total[:, :nlon]

    for r in range(2):
        lines = []
        for b in range(members):
            lines.append(jnp.dot(pick[r, b], weight[...], preferred_element_type=F32))
        mixer[r] = jnp.concatenate(lines, axis=1).astype(BF16)


def finish_rows(lower, present, edge, partial, kernel, table, mixer, slope, padded, act, taps):
    rows, depth, nlon = partial.shape
    size = kernel.shape[0]
    half = size // 2
    span = table.shape[1] // 2
    spread_taps(kernel, taps, False)
    for row in range(half):
        at = jnp.where(lower, row, half - 1 - row)
        value = joined(edge, at)
        if present is not None:
            value = jnp.where(present, value, jnp.zeros_like(value))
        fill_row(padded, row, value, half)

    @pl.loop(0, depth // TILE)
    def _(ct):
        c0 = pl.multiple_of(ct * TILE, TILE)
        for j in range(half):
            lines = [
                (row, jnp.where(lower, row - j, size - 1 - (row - j))) for row in range(j, half)
            ]
            at = jnp.where(lower, j, half - 1 - j)
            value = partial[jnp.where(lower, j, rows - 1 - j), pl.ds(c0, TILE), :]
            value = value + tap_sum(padded, taps, c0, lines, size)[:, :nlon]
            value, grad = gelu_pair(value)
            act[at, pl.ds(c0, TILE), :] = value.astype(BF16)
            slope[at, pl.ds(c0, TILE), :] = grad.astype(BF16)

    flat = act[...].reshape(half * depth, nlon)
    spectral = jnp.dot(flat, table[...], preferred_element_type=F32).astype(BF16)
    mixed = []
    for j in range(half):
        line = spectral[j * depth : (j + 1) * depth]
        mixed.append(
            jnp.dot(mixer[0], line[:, :span], preferred_element_type=F32)
            + jnp.dot(mixer[1], line[:, span:], preferred_element_type=F32)
        )
    return mixed


def near_kernel(flags, edge, partial, kernel, table, mixer, mixed, slope, padded, act, taps):
    lines = finish_rows(
        flags[0] == 1, None, edge, partial, kernel, table, mixer, slope, padded, act, taps
    )
    for j, line in enumerate(lines):
        mixed[j] = line.astype(BF16)


def far_kernel(share, flags, edge, partial, kernel, table, mixer, nearer, out, slope, padded, act, taps):
    owners, groups, height, lanes = out.shape
    lines = finish_rows(
        flags[0] != 1, flags[1] == 1, edge, partial, kernel, table, mixer, slope, padded, act, taps
    )
    lines = [nearer[j].astype(F32) for j in range(nearer.shape[0])] + lines
    for t in range(groups):
        pieces = [x[:, t * share : (t + 1) * share] for x in lines]
        if lanes > len(lines) * share:
            pieces.append(jnp.zeros((owners * height, lanes - len(lines) * share), F32))
        block = jnp.concatenate(pieces, axis=1)
        for e in range(owners):
            out[e, t] = block[e * height : (e + 1) * height].astype(BF16)


def flip_kernel(kernel, taps):
    spread_taps(kernel, taps, True)


def soft_sign(gaps):
    return gaps * lax.rsqrt(gaps * gaps + smooth_width * smooth_width)


def score_kernel(members, used, rows, halo, got, legendre, target, order, back, grads, spread, gather, picked):
    owners, groups, height, lanes = got.shape
    orders, nlat, degrees = legendre.shape
    slots = target.shape[1]
    ens = owners * members
    for t in range(groups):
        pieces = []
        for e in range(owners):
            block = got[e, t].astype(F32)
            for b in range(members):
                pieces.append(block[b * used : (b + 1) * used])
                if slots > used:
                    pieces.append(jnp.zeros((slots - used, lanes), F32))
        block = jnp.concatenate(pieces, axis=0).T
        at, part = t * rows * orders, halo * orders
        first, second = (at, at + part) if t % 2 else (at + part, at)
        spread[first : first + part, :] = block[:part]
        spread[second : second + part, :] = block[part : 2 * part]
    reorder = jnp.where(
        lax.broadcasted_iota(jnp.int32, (degrees, degrees), 0) == order[...], 1.0, 0.0
    )
    picked[...] = reorder.astype(BF16)
    edge = halo * orders
    gather[:edge, :] = jnp.zeros((edge, ens * slots), F32)
    gather[edge + nlat * orders :, :] = jnp.zeros((edge, ens * slots), F32)

    def score(values, truth):
        own = [values[k * slots : (k + 1) * slots] for k in range(ens)]
        sums = [None] * ens
        for k in range(ens):
            for n in range(k + 1, ens):
                sign = soft_sign(own[k] - own[n])
                sums[k] = sign if sums[k] is None else sums[k] + sign
                sums[n] = -sign if sums[n] is None else sums[n] - sign
        return jnp.concatenate(
            [
                soft_sign(own[k] - truth) * (1.0 / ens) - sums[k] * (1.0 / (ens * (ens - 1)))
                for k in range(ens)
            ],
            axis=0,
        )

    tail = degrees % 128
    packs = tail > 0 and 128 % tail == 0 and orders % (128 // tail) == 0
    step = 128 // tail if packs else 1
    body = degrees - tail if packs else degrees

    @pl.loop(0, orders // step)
    def _(trip):
        numbers = [trip * step + j for j in range(step)]
        coeffs = [
            lax.dot_general(
                spread[pl.ds(m, nlat, stride=orders), :].astype(BF16),
                legendre[m],
                (((0,), (0,)), ((), ())),
                preferred_element_type=F32,
            )
            for m in numbers
        ]
        truths = [target[m].astype(F32) for m in numbers]
        scored = [score(x[:, :body], y[:, :body]) for x, y in zip(coeffs, truths)]
        if packs:
            rest = score(
                jnp.concatenate([x[:, body:] for x in coeffs], axis=1),
                jnp.concatenate([y[:, body:] for y in truths], axis=1),
            )
            scored = [
                jnp.concatenate([x, rest[:, j * tail : (j + 1) * tail]], axis=1)
                for j, x in enumerate(scored)
            ]
        for m, grad in zip(numbers, scored):
            grad = grad.astype(BF16)
            gather[pl.ds(edge + m, nlat, stride=orders), :] = lax.dot_general(
                legendre[m], grad, (((1,), (1,)), ((), ())), preferred_element_type=F32
            )
            at = pl.multiple_of(m * ens * slots, 8)
            ordered = jnp.dot(grad, picked[...], preferred_element_type=F32)
            for j in range(grads.shape[0]):
                last = min(degrees, (j + 1) * 128)
                grads[j, pl.ds(at, ens * slots), : last - j * 128] = ordered[:, j * 128 : last].astype(BF16)

    wide = back.shape[3]
    tall = (rows + 2 * halo) * orders
    for t in range(groups):
        at = t * rows * orders
        block = gather[at : at + tall, :]
        if wide > tall:
            block = jnp.concatenate([block, jnp.zeros((wide - tall, ens * slots), F32)], axis=0)
        block = block.T
        for e in range(owners):
            pieces = []
            for b in range(members):
                at = (e * members + b) * slots
                pieces.append(block[at : at + used])
            if height > members * used:
                pieces.append(jnp.zeros((height - members * used, wide), F32))
            back[e, t] = jnp.concatenate(pieces, axis=0).astype(BF16)


def backward_kernel(share, flags, got, near, far, inner, outer, taps, mixer, table, out, padded, flat, stage):
    owners, groups, height, _ = got.shape
    half, depth, nlon = inner.shape
    members, rows, chans, _ = out.shape
    size = math.isqrt(taps.shape[0])
    span = table.shape[1] // 2
    total = rows + 2 * half
    blocks = [
        jnp.concatenate([got[e, t].astype(F32) for e in range(owners)], axis=0) for t in range(groups)
    ]
    lines = []
    for i in range(total):
        pieces = [x[:, i * share : (i + 1) * share] for x in blocks]
        pieces.append(jnp.zeros((owners * height, span - groups * share), F32))
        line = jnp.concatenate(pieces, axis=1).astype(BF16)
        lines.append(
            jnp.concatenate(
                [
                    lax.dot_general(
                        mixer[r], line, (((0,), (0,)), ((), ())), preferred_element_type=F32
                    ).astype(BF16)
                    for r in range(2)
                ],
                axis=1,
            )
        )
    flat[...] = lax.dot_general(
        jnp.concatenate(lines, axis=0),
        table[...],
        (((1,), (1,)), ((), ())),
        preferred_element_type=F32,
    ).reshape(flat.shape)
    odd = flags[0] == 1
    pairs = ((near, far), (inner, outer), (outer, inner), (far, near))
    for part, (one, other) in enumerate(pairs):
        for row in range(half):
            at = part * half + row
            slope = jnp.where(odd, one[row].astype(F32), other[row].astype(F32))
            fill_row(padded, at, flat[at] * slope, half)

    @pl.loop(0, depth // TILE)
    def _(ct):
        c0 = pl.multiple_of(ct * TILE, TILE)

        @pl.loop(0, rows)
        def _(i):
            value = tap_sum(padded, taps, c0, [(i + p, p) for p in range(size)], size)
            value = value + padded[i + half, pl.ds(c0, TILE), :].astype(F32)
            stage[i, pl.ds(c0, TILE), :] = value[:, :nlon]

    for b in range(members):
        for i in range(rows):
            out[b, i] = stage[i, b * chans : (b + 1) * chans, :].astype(BF16)


def pack_kernel(members, used, per_owner, rounded, out, grads):
    owners, groups, depth, lanes = out.shape
    share = depth // members
    stride = grads.shape[1] // share
    grads[...] = rounded[...].astype(F32)
    slots = stride // (owners * members)
    for e in range(owners):
        for b in range(members):
            at = (e * members + b) * slots
            planes = [
                jnp.concatenate(
                    [grads[j, pl.ds(at + s, share, stride=stride), :] for j in range(grads.shape[0])],
                    axis=1,
                )
                for s in range(used)
            ]
            for t in range(groups):
                pieces = [x[:, t * per_owner : (t + 1) * per_owner] for x in planes]
                if lanes > used * per_owner:
                    pieces.append(jnp.zeros((share, lanes - used * per_owner), F32))
                out[e, t, b * share : (b + 1) * share, :] = jnp.concatenate(pieces, axis=1).astype(BF16)


def unpack_kernel(members, got, out):
    owners, groups, depth, lanes = got.shape
    _, chans, per_owner, _, orders = out.shape
    share, chan_share = depth // members, chans // owners
    pair = 2 * per_owner

    def iotas(shape):
        return (lax.broadcasted_iota(jnp.int32, shape, d) for d in range(2))

    row, column = iotas((chan_share * pair, lanes))
    wanted = ((row % 2) * chan_share + row // pair) * per_owner + (row % pair) // 2
    swapped = jnp.where(column == wanted, 1.0, 0.0).astype(BF16)
    row, column = iotas((groups * depth, orders))
    start = (column // share) * depth + column % share
    pickers = [jnp.where(row == start + b * share, 1.0, 0.0).astype(BF16) for b in range(members)]
    for e in range(owners):
        turned = lax.dot_general(
            swapped,
            got[e].reshape(groups * depth, lanes),
            (((1,), (1,)), ((), ())),
            preferred_element_type=F32,
        ).astype(BF16)
        for b in range(members):
            lines = jnp.dot(turned, pickers[b], preferred_element_type=F32)
            for c in range(chan_share):
                block = lines[c * pair : (c + 1) * pair]
                out[b, e * chan_share + c] = block.reshape(per_owner, 2, orders)


def local(fields, depth_kernel, mix_weight, legendre, truth, degree_order):
    ens_parts, groups = lax.axis_size("ens"), lax.axis_size("lat")
    ens_at, lat_at = lax.axis_index("ens"), lax.axis_index("lat")
    members, chans, rows, nlon = fields.shape
    _, orders, degrees = legendre.shape
    ens = members * ens_parts
    nlat = rows * groups
    share, per_owner, chan_share = orders // groups, degrees // groups, chans // ens_parts
    used = 2 * chan_share
    slots = up(used, 8)
    height = up(members * used, 8)
    span = up(orders, 128)
    size = depth_kernel.shape[1]
    halo = size // 2
    wide = up(nlon + 2 * halo, 128)
    depth = members * chans

    table = jnp.asarray(wave_table(nlon, orders, span))
    kernel = depth_kernel.transpose(1, 2, 0)
    flags = place()
    own = fields.transpose(0, 2, 1, 3)
    odd = lat_at % 2
    near, far = partners(
        lax.dynamic_slice_in_dim(own, (1 - odd) * (rows - halo), halo, 1),
        lax.dynamic_slice_in_dim(own, odd * (rows - halo), halo, 1),
    )

    pick = np.zeros((2, members, ens_parts, height, chans), np.float32)
    for r in range(2):
        for b in range(members):
            for o in range(chans):
                at = b * used + r * chan_share + o % chan_share
                pick[r, b, o // chan_share, at, o] = 1.0
    pick = jnp.asarray(pick.reshape(2, members, ens_parts * height, chans).astype(jnp.bfloat16))

    def grant(mebibytes):
        return pltpu.CompilerParams(vmem_limit_bytes=mebibytes * 1024 * 1024)

    scalars = pl.BlockSpec(memory_space=pltpu.SMEM)
    whole = pl.BlockSpec(memory_space=pltpu.VMEM)
    grid_shape = (members, rows, chans, nlon)
    lined = jax.ShapeDtypeStruct((rows, depth, nlon), F32)
    edge = jax.ShapeDtypeStruct((halo, depth, nlon), BF16)
    taps_out = jax.ShapeDtypeStruct((size * size, depth, 128), BF16)

    def call(body, outs, scratch, name, work, *args):
        specs = [scalars if a is flags else whole for a in args]
        return pl.pallas_call(
            body,
            out_shape=outs,
            in_specs=specs,
            scratch_shapes=scratch,
            compiler_params=grant(60 if name in ("prepare", "nearer", "farther") else 28),
            cost_estimate=pl.CostEstimate(
                flops=work, transcendentals=0, bytes_accessed=8 * rows * depth * nlon
            ),
        )(*args)

    def swap(x):
        flat = x.reshape((ens_parts * groups,) + x.shape[2:])
        flat = lax.all_to_all(flat, ("ens", "lat"), split_axis=0, concat_axis=0, tiled=True)
        return flat.reshape(x.shape)

    work = 2 * size * size * rows * depth * nlon
    partial, mixer = call(
        prepare_kernel,
        (lined, jax.ShapeDtypeStruct((2, ens_parts * height, depth), BF16)),
        [pltpu.VMEM((rows, depth, wide), BF16), pltpu.VMEM(taps_out.shape, BF16)],
        "prepare",
        work,
        own,
        kernel,
        mix_weight,
        pick,
    )
    target = lax.dynamic_slice(
        truth, (ens_at * chan_share, 0, lat_at * share, 0), (chan_share, 2, share, degrees)
    )
    target = target.transpose(2, 1, 0, 3).reshape(share, used, degrees)
    target = jnp.pad(target, ((0, 0), (0, slots - used), (0, 0)))

    slab = legendre.reshape(rows, groups, share * degrees).transpose(1, 0, 2)
    line = math.gcd(rows * share * degrees, 128)
    slab = slab.reshape(groups, rows * share * degrees // line, line)

    def chunk(lines):
        return jax.ShapeDtypeStruct((ens_parts, groups, height, up(lines * share, 128)), BF16)

    half_scratch = [
        pltpu.VMEM((halo, depth, wide), BF16),
        pltpu.VMEM((halo, depth, nlon), BF16),
        pltpu.VMEM(taps_out.shape, BF16),
    ]
    mixed, inner = call(
        near_kernel,
        (jax.ShapeDtypeStruct((halo, ens_parts * height, span), BF16), edge),
        half_scratch,
        "nearer",
        work // 2,
        flags,
        near,
        partial,
        kernel,
        table,
        mixer,
    )
    slab, mixed = lax.optimization_barrier((slab, mixed))
    slab = lax.all_to_all(slab, "lat", split_axis=0, concat_axis=0, tiled=True)
    order_legendre = slab.reshape(nlat, share, degrees).transpose(1, 0, 2)
    sent, outer = call(
        functools.partial(far_kernel, share),
        (chunk(rows), edge),
        half_scratch,
        "farther",
        work // 2,
        flags,
        far,
        partial,
        kernel,
        table,
        mixer,
        mixed,
    )
    got = swap(sent)
    got, held = lax.optimization_barrier((got, outer))
    near, far = partners(inner, held)
    back, grads = call(
        functools.partial(score_kernel, members, used, rows, halo),
        (
            chunk(rows + 2 * halo),
            jax.ShapeDtypeStruct((up(degrees, 128) // 128, share * ens * slots, 128), BF16),
        ),
        [
            pltpu.VMEM((nlat * share, ens * slots), F32),
            pltpu.VMEM(((nlat + 2 * halo) * share, ens * slots), F32),
            pltpu.VMEM((degrees, degrees), BF16),
        ],
        "score",
        work,
        got,
        order_legendre,
        target,
        degree_order.reshape(1, degrees),
    )
    returned = swap(back)
    packed = call(
        functools.partial(pack_kernel, members, used, per_owner),
        jax.ShapeDtypeStruct(
            (ens_parts, groups, members * share, up(used * per_owner, 128)), BF16
        ),
        [pltpu.VMEM(grads.shape, F32)],
        "pack",
        work,
        grads,
    )
    owned = swap(packed)
    flipped = call(flip_kernel, taps_out, [], "flip", work // 8, kernel)
    grad_fields = call(
        functools.partial(backward_kernel, share),
        jax.ShapeDtypeStruct(grid_shape, BF16),
        [
            pltpu.VMEM((rows + 2 * halo, depth, wide), BF16),
            pltpu.VMEM((rows + 2 * halo, depth, nlon), F32),
            pltpu.VMEM((rows, depth, nlon), F32),
        ],
        "backward",
        work,
        flags,
        returned,
        near,
        far,
        inner,
        outer,
        flipped,
        mixer,
        table,
    )
    score_grad = call(
        functools.partial(unpack_kernel, members),
        jax.ShapeDtypeStruct((members, chans, per_owner, 2, orders), F32),
        [],
        "unpack",
        work,
        owned,
    )
    return grad_fields.transpose(0, 2, 1, 3), score_grad.transpose(0, 1, 3, 4, 2)


def solution(mesh):
    placed = (P("ens", None, "lat", None), P(), P(), P("lat", None, None), P(), P())

    return jax.shard_map(
        local,
        mesh=mesh,
        in_specs=placed,
        out_specs=(P("ens", None, "lat", None), P("ens", None, None, None, "lat")),
        check_vma=False,
    )
```

profile of v0, /device:TPU:0, one launch (start us, length us, event | category | flops | bytes accessed | tf_op | source)
XLA Modules:
  0.0 128.5 jit_solution(13815230109191664055)
XLA Ops:
  0.7 1.3 dynamic-slice_bitcast_fusion
  1.9 3.1 %collective-permute-start.1 = (bf16[2,3,24,1440]{3,2,1,0:T(8,128)(2,1)S(1)}, bf16[2,3,24,1440]{3,2,1,0:T(8,128)(2,1)S(1)}, u32[]{:S(2)}, u32[]{:S(2)}) collective-permute-start(bf16[2,3,24,1440]{3,2,1,0:T(8,128)(2,1)S(1)} %get-tuple-element.26), channel_id=1, source_target_pairs={{0,1},{1,0},{2,3},{3,2},{4,5},{5,4},{6,7},{7,6},{8,9},{9,8},{10,11... | collective-permute-start | bytes 1244168 | tf_op jit(solution)/shard_map/ppermute | solution.py:37
  6.3 6.5 %shard_map.95 = (f32[6,48,1440]{2,1,0:T(8,128)}, bf16[2,96,48]{2,1,0:T(8,128)(2,1)}) custom-call(bf16[2,6,24,1440]{3,2,1,0:T(8,128)(2,1)} %bitcast.35, f32[7,7,24]{2,1,0:T(8,128)} %bitcast.30, bf16[24,24]{1,0:T(8,128)(2,1)} %weight.1, bf16[2,2,96,24]{3,2,1,0:T(8,128)(2,1)} %constant.44.clone.pick), custom_call_target="tpu_custom_call" | custom-call | flops 40642560 | bytes 3317760 | tf_op jit(solution)/shard_map/pallas_call | solution.py:449
  13.4 10.5 %collective-permute-done.1.edge = bf16[2,3,24,1440]{3,2,1,0:T(8,128)(2,1)S(1)} collective-permute-done((bf16[2,3,24,1440]{3,2,1,0:T(8,128)(2,1)S(1)}, bf16[2,3,24,1440]{3,2,1,0:T(8,128)(2,1)S(1)}, u32[]{:S(2)}, u32[]{:S(2)}) %collective-permute-start.1) | collective-permute-done | bytes 414752 | tf_op jit(solution)/shard_map/ppermute | solution.py:37
  24.7 5.3 %shard_map.96 = (bf16[3,96,256]{2,1,0:T(8,128)(2,1)}, bf16[3,48,1440]{2,1,0:T(8,128)(2,1)}) custom-call(s32[2]{0:T(128)} %pad_add_fusion.flags, bf16[2,3,24,1440]{3,2,1,0:T(8,128)(2,1)} %copy-done.11, f32[6,48,1440]{2,1,0:T(8,128)} %get-tuple-element.14.partial, f32[7,7,24]{2,1,0:T(8,128)} %bitcast.31, bf16[1440,512]{1,0:T(8,128)(2,1)} %constant.43.clone.table, ...), custom_call_target="tpu_custom_call" | custom-call | flops 20321280 | bytes 3317760 | tf_op jit(solution)/shard_map/pallas_call | solution.py:449
  30.7 5.6 %shard_map.97 = (bf16[4,8,24,128]{3,2,1,0:T(8,128)(2,1)}, bf16[3,48,1440]{2,1,0:T(8,128)(2,1)}) custom-call(s32[2]{0:T(128)} %pad_add_fusion.flags, bf16[2,3,24,1440]{3,2,1,0:T(8,128)(2,1)} %copy-done.10, f32[6,48,1440]{2,1,0:T(8,128)} %get-tuple-element.14.partial, f32[7,7,24]{2,1,0:T(8,128)} %bitcast.32, bf16[1440,512]{1,0:T(8,128)(2,1)} %constant.43.clone.table, ...), custom_call_target="tpu_custom_call" | custom-call | flops 20321280 | bytes 3317760 | tf_op jit(solution)/shard_map/pallas_call | solution.py:449
  36.3 5.9 %all-to-all-start = ((bf16[32,24,128]{2,1,0:T(8,128)(2,1)}), bf16[32,24,128]{2,1,0:T(8,128)(2,1)S(1)}, u32[]{:S(2)}, u32[]{:S(2)}) async-start(bf16[32,24,128]{2,1,0:T(8,128)(2,1)} %bitcast.40), calls=%async_computation | async-start | bytes 393216 | tf_op jit(solution)/shard_map/all_to_all | solution.py:462
  42.2 0.8 copy.15
  43.0 7.5 %all-to-all-done = bf16[32,24,128]{2,1,0:T(8,128)(2,1)S(1)} async-done(((bf16[32,24,128]{2,1,0:T(8,128)(2,1)}), bf16[32,24,128]{2,1,0:T(8,128)(2,1)S(1)}, u32[]{:S(2)}, u32[]{:S(2)}) %all-to-all-start) | async-done | bytes 196640 | tf_op jit(solution)/shard_map/all_to_all | solution.py:462
  50.4 4.2 %all-to-all-start.1 = ((bf16[8,150,128]{2,1,0:T(8,128)(2,1)}), bf16[8,150,128]{2,1,0:T(8,128)(2,1)S(1)}, u32[]{:S(2)}, u32[]{:S(2)}) async-start(bf16[8,150,128]{2,1,0:T(8,128)(2,1)} %copy.15), calls=%async_computation.1 | async-start | bytes 622592 | tf_op jit(solution)/shard_map/all_to_all | solution.py:509
  54.6 1.0 constant_dynamic-slice_fusion
  55.7 8.9 %all-to-all-done.1 = bf16[8,150,128]{2,1,0:T(8,128)(2,1)S(1)} async-done(((bf16[8,150,128]{2,1,0:T(8,128)(2,1)}), bf16[8,150,128]{2,1,0:T(8,128)(2,1)S(1)}, u32[]{:S(2)}, u32[]{:S(2)}) %all-to-all-start.1) | async-done | bytes 307232 | tf_op jit(solution)/shard_map/all_to_all | solution.py:509
  65.4 4.7 %shard_map.98 = (bf16[4,8,24,256]{3,2,1,0:T(8,128)(2,1)}, bf16[2,2560,128]{2,1,0:T(8,128)(2,1)S(1)}) custom-call(bf16[4,8,24,128]{3,2,1,0:T(8,128)(2,1)S(1)} %bitcast.29, bf16[20,48,160]{2,1,0:T(8,128)(2,1)S(1)} %bitcast.27, bf16[20,16,160]{2,1,0:T(8,128)(2,1)S(1)} %pad.4.target, s32[1,160]{1,0:T(1,128)S(1)} %bitcast.34), custom_call_target="tpu_custom_call" | custom-call | flops 40642560 | bytes 3317760 | tf_op jit(solution)/shard_map/pallas_call | solution.py:449
  70.1 1.1 copy-done.1
  71.2 3.6 %all-to-all-start.2 = ((bf16[32,24,256]{2,1,0:T(8,128)(2,1)}), bf16[32,24,256]{2,1,0:T(8,128)(2,1)S(1)}, u32[]{:S(2)}, u32[]{:S(2)}) async-start(bf16[32,24,256]{2,1,0:T(8,128)(2,1)} %bitcast.14), calls=%async_computation.2 | async-start | bytes 786432 | tf_op jit(solution)/shard_map/all_to_all | solution.py:462
  74.8 1.4 %copy-done.2 = bf16[2,2560,128]{2,1,0:T(8,128)(2,1)S(1)} copy-done((bf16[2,2560,128]{2,1,0:T(8,128)(2,1)S(1)}, bf16[2,2560,128]{2,1,0:T(8,128)(2,1)}, u32[]{:S(2)}) %copy-start.2) | copy-done | bytes 1310744
  76.2 2.7 %shard_map.101 = bf16[4,8,40,256]{3,2,1,0:T(8,128)(2,1)} custom-call(bf16[2,2560,128]{2,1,0:T(8,128)(2,1)S(1)} %copy-done.2), custom_call_target="tpu_custom_call" | custom-call | flops 40642560 | bytes 3317760 | tf_op jit(solution)/shard_map/pallas_call | solution.py:449
  78.9 9.3 %all-to-all-done.2 = bf16[32,24,256]{2,1,0:T(8,128)(2,1)S(1)} async-done(((bf16[32,24,256]{2,1,0:T(8,128)(2,1)}), bf16[32,24,256]{2,1,0:T(8,128)(2,1)S(1)}, u32[]{:S(2)}, u32[]{:S(2)}) %all-to-all-start.2) | async-done | bytes 393248 | tf_op jit(solution)/shard_map/all_to_all | solution.py:462
  88.2 2.6 %all-to-all-start.3 = ((bf16[32,40,256]{2,1,0:T(8,128)(2,1)}), bf16[32,40,256]{2,1,0:T(8,128)(2,1)S(1)}, u32[]{:S(2)}, u32[]{:S(2)}) async-start(bf16[32,40,256]{2,1,0:T(8,128)(2,1)} %bitcast.17), calls=%async_computation.3 | async-start | bytes 1310720 | tf_op jit(solution)/shard_map/all_to_all | solution.py:462
  90.8 1.7 %collective-permute-start.2 = (bf16[3,48,1440]{2,1,0:T(8,128)(2,1)S(1)}, bf16[3,48,1440]{2,1,0:T(8,128)(2,1)S(1)}, u32[]{:S(2)}, u32[]{:S(2)}) collective-permute-start(bf16[3,48,1440]{2,1,0:T(8,128)(2,1)S(1)} %copy-done.5), channel_id=1, source_target_pairs={{0,1},{1,0},{2,3},{3,2},{4,5},{5,4},{6,7},{7,6},{8,9},{9,8},{10,11... | collective-permute-start | bytes 1244168 | tf_op jit(solution)/shard_map/ppermute | solution.py:37
  92.6 0.9 collective-permute-start.3
  93.7 23.9 %collective-permute-done.2.near = bf16[3,48,1440]{2,1,0:T(8,128)(2,1)S(1)} collective-permute-done((bf16[3,48,1440]{2,1,0:T(8,128)(2,1)S(1)}, bf16[3,48,1440]{2,1,0:T(8,128)(2,1)S(1)}, u32[]{:S(2)}, u32[]{:S(2)}) %collective-permute-start.2) | collective-permute-done | bytes 414752 | tf_op jit(solution)/shard_map/ppermute | solution.py:37
  117.6 8.2 %shard_map.100 = bf16[2,6,24,1440]{3,2,1,0:T(8,128)(2,1)} custom-call(s32[2]{0:T(128)S(1)} %copy-done.7, bf16[4,8,24,256]{3,2,1,0:T(8,128)(2,1)S(1)} %bitcast.28, bf16[3,48,1440]{2,1,0:T(8,128)(2,1)S(1)} %collective-permute-done.2.near, bf16[3,48,1440]{2,1,0:T(8,128)(2,1)S(1)} %collective-permute-done.3.far, bf16[3,48,1440]{2,1,0:T(8,128)(2,1)S(1)} %copy-done.5, ...), custom_call_target="tpu_custom_call" | custom-call | flops 40642560 | bytes 3317760 | tf_op jit(solution)/shard_map/pallas_call | solution.py:449
  125.9 2.6 %shard_map.102 = f32[2,24,20,2,160]{4,3,2,1,0:T(2,128)} custom-call(bf16[4,8,40,256]{3,2,1,0:T(8,128)(2,1)S(1)} %bitcast.26), custom_call_target="tpu_custom_call" | custom-call | flops 40642560 | bytes 3317760 | tf_op jit(solution)/shard_map/pallas_call | solution.py:449
  (34 shorter events, 4.6 us)
Async XLA Ops:
  0.6 5.1 %copy-start.9 = (bf16[6,160,160]{2,1,0:T(8,128)(2,1)S(1)}, bf16[6,160,160]{2,1,0:T(8,128)(2,1)}, u32[]{:S(2)}) copy-start(bf16[6,160,160]{2,1,0:T(8,128)(2,1)} %param.11) | copy-start | bytes 921604
  1.9 22.0 %collective-permute-start.1 = (bf16[2,3,24,1440]{3,2,1,0:T(8,128)(2,1)S(1)}, bf16[2,3,24,1440]{3,2,1,0:T(8,128)(2,1)S(1)}, u32[]{:S(2)}, u32[]{:S(2)}) collective-permute-start(bf16[2,3,24,1440]{3,2,1,0:T(8,128)(2,1)S(1)} %get-tuple-element.26), channel_id=1, source_target_pairs={{0,1},{1,0},{2,3},{3,2},{4,5},{5,4},{6,7},{7,6},{8,9},{9,8},{10,11... | collective-permute-start | bytes 1244168 | tf_op jit(solution)/shard_map/ppermute | solution.py:37
  5.0 25.0 %collective-permute-start = (bf16[2,3,24,1440]{3,2,1,0:T(8,128)(2,1)S(1)}, bf16[2,3,24,1440]{3,2,1,0:T(8,128)(2,1)S(1)}, u32[]{:S(2)}, u32[]{:S(2)}) collective-permute-start(bf16[2,3,24,1440]{3,2,1,0:T(8,128)(2,1)S(1)} %get-tuple-element.27), channel_id=1, source_target_pairs={{0,0},{1,2},{2,1},{3,4},{4,3},{5,6},{6,5},{7,7},{8,8},{9,10},{10,9... | collective-permute-start | bytes 1244168 | tf_op jit(solution)/shard_map/ppermute | solution.py:38
  23.9 0.8 copy-start.11
  30.0 0.8 copy-start.10
  36.3 14.1 %all-to-all-start = ((bf16[32,24,128]{2,1,0:T(8,128)(2,1)}), bf16[32,24,128]{2,1,0:T(8,128)(2,1)S(1)}, u32[]{:S(2)}, u32[]{:S(2)}) async-start(bf16[32,24,128]{2,1,0:T(8,128)(2,1)} %bitcast.40), calls=%async_computation | async-start | bytes 393216 | tf_op jit(solution)/shard_map/all_to_all | solution.py:462
  43.0 22.4 %copy-start.8 = (s32[160]{0:T(256)S(1)}, s32[160]{0:T(256)}, u32[]{:S(2)}) copy-start(s32[160]{0:T(256)} %param.13) | copy-start | bytes 1924
  50.4 14.2 %all-to-all-start.1 = ((bf16[8,150,128]{2,1,0:T(8,128)(2,1)}), bf16[8,150,128]{2,1,0:T(8,128)(2,1)S(1)}, u32[]{:S(2)}, u32[]{:S(2)}) async-start(bf16[8,150,128]{2,1,0:T(8,128)(2,1)} %copy.15), calls=%async_computation.1 | async-start | bytes 622592 | tf_op jit(solution)/shard_map/all_to_all | solution.py:509
  70.1 1.1 copy-start.1
  71.1 19.7 %copy-start.5 = (bf16[3,48,1440]{2,1,0:T(8,128)(2,1)S(1)}, bf16[3,48,1440]{2,1,0:T(8,128)(2,1)}, u32[]{:S(2)}) copy-start(bf16[3,48,1440]{2,1,0:T(8,128)(2,1)} %get-tuple-element.23.inner) | copy-start | bytes 1244164
  71.1 22.3 %copy-start.3 = (f32[24,7,7]{0,2,1:T(8,128)S(1)}, f32[24,7,7]{0,2,1:T(8,128)}, u32[]{:S(2)}) copy-start(f32[24,7,7]{0,2,1:T(8,128)} %param.9) | copy-start | bytes 14116
  71.2 17.1 %all-to-all-start.2 = ((bf16[32,24,256]{2,1,0:T(8,128)(2,1)}), bf16[32,24,256]{2,1,0:T(8,128)(2,1)S(1)}, u32[]{:S(2)}, u32[]{:S(2)}) async-start(bf16[32,24,256]{2,1,0:T(8,128)(2,1)} %bitcast.14), calls=%async_computation.2 | async-start | bytes 786432 | tf_op jit(solution)/shard_map/all_to_all | solution.py:462
  74.8 42.8 %copy-start = (bf16[1440,512]{1,0:T(8,128)(2,1)S(1)}, bf16[1440,512]{1,0:T(8,128)(2,1)}, u32[]{:S(2)}) copy-start(bf16[1440,512]{1,0:T(8,128)(2,1)} %constant.43.clone.table) | copy-start | bytes 4423684
  74.8 1.4 %copy-start.2 = (bf16[2,2560,128]{2,1,0:T(8,128)(2,1)S(1)}, bf16[2,2560,128]{2,1,0:T(8,128)(2,1)}, u32[]{:S(2)}) copy-start(bf16[2,2560,128]{2,1,0:T(8,128)(2,1)} %copy-done.1) | copy-start | bytes 3932164
  76.2 16.3 %copy-start.6 = (bf16[3,48,1440]{2,1,0:T(8,128)(2,1)S(1)}, bf16[3,48,1440]{2,1,0:T(8,128)(2,1)}, u32[]{:S(2)}) copy-start(bf16[3,48,1440]{2,1,0:T(8,128)(2,1)} %get-tuple-element.24.outer) | copy-start | bytes 1244164
  76.2 41.4 %copy-start.4 = (bf16[2,96,48]{2,1,0:T(8,128)(2,1)S(1)}, bf16[2,96,48]{2,1,0:T(8,128)(2,1)}, u32[]{:S(2)}) copy-start(bf16[2,96,48]{2,1,0:T(8,128)(2,1)} %get-tuple-element.15.mixer) | copy-start | bytes 55300
  76.2 41.4 %copy-start.7 = (s32[2]{0:T(128)S(1)}, s32[2]{0:T(128)}, u32[]{:S(2)}) copy-start(s32[2]{0:T(128)} %pad_add_fusion.flags) | copy-start | bytes 28
  88.2 37.7 %all-to-all-start.3 = ((bf16[32,40,256]{2,1,0:T(8,128)(2,1)}), bf16[32,40,256]{2,1,0:T(8,128)(2,1)S(1)}, u32[]{:S(2)}, u32[]{:S(2)}) async-start(bf16[32,40,256]{2,1,0:T(8,128)(2,1)} %bitcast.17), calls=%async_computation.3 | async-start | bytes 1310720 | tf_op jit(solution)/shard_map/all_to_all | solution.py:462
  90.8 26.8 %collective-permute-start.2 = (bf16[3,48,1440]{2,1,0:T(8,128)(2,1)S(1)}, bf16[3,48,1440]{2,1,0:T(8,128)(2,1)S(1)}, u32[]{:S(2)}, u32[]{:S(2)}) collective-permute-start(bf16[3,48,1440]{2,1,0:T(8,128)(2,1)S(1)} %copy-done.5), channel_id=1, source_target_pairs={{0,1},{1,0},{2,3},{3,2},{4,5},{5,4},{6,7},{7,6},{8,9},{9,8},{10,11... | collective-permute-start | bytes 1244168 | tf_op jit(solution)/shard_map/ppermute | solution.py:37
  92.6 25.1 %collective-permute-start.3 = (bf16[3,48,1440]{2,1,0:T(8,128)(2,1)S(1)}, bf16[3,48,1440]{2,1,0:T(8,128)(2,1)S(1)}, u32[]{:S(2)}, u32[]{:S(2)}) collective-permute-start(bf16[3,48,1440]{2,1,0:T(8,128)(2,1)S(1)} %copy-done.6), channel_id=1, source_target_pairs={{0,0},{1,2},{2,1},{3,4},{4,3},{5,6},{6,5},{7,7},{8,8},{9,10},{10,9... | collective-permute-start | bytes 1244168 | tf_op jit(solution)/shard_map/ppermute | solution.py:38
where the time goes:
time: 130 us; the launch traced here: 128 us
  waiting for transfers between devices  60.2 us (46%)
  Pallas kernels  35.8 us (28%)
  starting transfers between devices  22.6 us (17%)
  local copies, waits for them, and re-layouts  8.53 us (7%)
    pallas_call x8, Pallas kernels, call(): pl.pallas_call(body, out_shape=outs, in_specs=specs, scratch_shapes=scrat...  35.8 us
    ppermute x2, waiting for transfers between devices, partners(): one = lax.ppermute(inner, 'lat', near)  34.4 us
    all_to_all x3, waiting for transfers between devices, swap(): lax.all_to_all(flat, ('ens', 'lat'), split_axis=0, concat_axis=0, tiled=T...  16.8 us
    all_to_all x3, starting transfers between devices, swap(): lax.all_to_all(flat, ('ens', 'lat'), split_axis=0, concat_axis=0, tiled=T...  12.1 us
    all_to_all x1, waiting for transfers between devices, local(): slab = lax.all_to_all(slab, 'lat', split_axis=0, concat_axis=0, tiled=True)  8.93 us
    ppermute x2, starting transfers between devices, partners(): one = lax.ppermute(inner, 'lat', near)  4.78 us
    all_to_all x1, starting transfers between devices, local(): slab = lax.all_to_all(slab, 'lat', split_axis=0, concat_axis=0, tiled=True)  4.17 us
    unnamed x25, local copies, waits for them, and re-layouts  4.04 us
  transfers between devices with their start and end apart: 8, of which 5 were waited for; matrix products, arithmetic and copies ran while one was open for 2% of the time, Pallas kernels for 18%

commit v1 on v0

--- a/solution.py
+++ b/solution.py
@@ -33,7 +33,7 @@
 def partners(inner, outer):
     count = lax.axis_size("lat")
     near = [(i, i ^ 1) for i in range(count)]
-    far = [(i, min(max(i + (1 if i % 2 else -1), 0), count - 1)) for i in range(count)]
+    far = [(i, (i + (1 if i % 2 else -1)) % count) for i in range(count)]
     one = lax.ppermute(inner, "lat", near)
     other = lax.ppermute(outer, "lat", far)
     return one, other
@@ -193,7 +193,7 @@
     return gaps * lax.rsqrt(gaps * gaps + smooth_width * smooth_width)
 
 
-def score_kernel(members, used, rows, halo, got, legendre, target, order, back, grads, spread, gather, picked):
+def score_kernel(members, used, rows, halo, got, legendre, target, order, back, drained, spread, gather, picked, grads, sent):
     owners, groups, height, lanes = got.shape
     orders, nlat, degrees = legendre.shape
     slots = target.shape[1]
@@ -239,6 +239,12 @@
     packs = tail > 0 and 128 % tail == 0 and orders % (128 // tail) == 0
     step = 128 // tail if packs else 1
     body = degrees - tail if packs else degrees
+
+    span = step * ens * slots
+
+    def drain(trip):
+        lines = pl.ds(pl.multiple_of(trip * span, 8), span)
+        return pltpu.make_async_copy(grads.at[:, lines], drained.at[:, lines], sent.at[trip])
 
     @pl.loop(0, orders // step)
     def _(trip):
@@ -273,6 +279,7 @@
             for j in range(grads.shape[0]):
                 last = min(degrees, (j + 1) * 128)
                 grads[j, pl.ds(at, ens * slots), : last - j * 128] = ordered[:, j * 128 : last].astype(BF16)
+        drain(trip).start()
 
     wide = back.shape[3]
     tall = (rows + 2 * halo) * orders
@@ -290,6 +297,10 @@
             if height > members * used:
                 pieces.append(jnp.zeros((height - members * used, wide), F32))
             back[e, t] = jnp.concatenate(pieces, axis=0).astype(BF16)
+
+    @pl.loop(0, orders // step)
+    def _(trip):
+        drain(trip).wait()
 
 
 def backward_kernel(share, flags, got, near, far, inner, outer, taps, mixer, table, out, padded, flat, stage):
@@ -370,7 +381,7 @@
                 out[e, t, b * share : (b + 1) * share, :] = jnp.concatenate(pieces, axis=1).astype(BF16)
 
 
-def unpack_kernel(members, got, out):
+def unpack_kernel(members, got, result, out, sent):
     owners, groups, depth, lanes = got.shape
     _, chans, per_owner, _, orders = out.shape
     share, chan_share = depth // members, chans // owners
@@ -385,6 +396,7 @@
     row, column = iotas((groups * depth, orders))
     start = (column // share) * depth + column % share
     pickers = [jnp.where(row == start + b * share, 1.0, 0.0).astype(BF16) for b in range(members)]
+    copies = []
     for e in range(owners):
         turned = lax.dot_general(
             swapped,
@@ -397,6 +409,13 @@
             for c in range(chan_share):
                 block = lines[c * pair : (c + 1) * pair]
                 out[b, e * chan_share + c] = block.reshape(per_owner, 2, orders)
+            place = pl.ds(e * chan_share, chan_share)
+            copies.append(
+                pltpu.make_async_copy(out.at[b, place], result.at[b, place], sent.at[e, b])
+            )
+            copies[-1].start()
+    for copy in copies:
+        copy.wait()
 
 
 def local(fields, depth_kernel, mix_weight, legendre, truth, degree_order):
@@ -444,18 +463,25 @@
     edge = jax.ShapeDtypeStruct((halo, depth, nlon), BF16)
     taps_out = jax.ShapeDtypeStruct((size * size, depth, 128), BF16)
 
-    def call(body, outs, scratch, name, work, *args):
+    def call(body, outs, scratch, name, work, *args, drained=()):
+        outs = outs if isinstance(outs, tuple) else (outs,)
+        places = [
+            pl.BlockSpec(memory_space=pltpu.HBM if i in drained else pltpu.VMEM)
+            for i in range(len(outs))
+        ]
         specs = [scalars if a is flags else whole for a in args]
-        return pl.pallas_call(
+        made = pl.pallas_call(
             body,
             out_shape=outs,
             in_specs=specs,
+            out_specs=tuple(places),
             scratch_shapes=scratch,
             compiler_params=grant(60 if name in ("prepare", "nearer", "farther") else 28),
             cost_estimate=pl.CostEstimate(
                 flops=work, transcendentals=0, bytes_accessed=8 * rows * depth * nlon
             ),
         )(*args)
+        return made if len(outs) > 1 else made[0]
 
     def swap(x):
         flat = x.reshape((ens_parts * groups,) + x.shape[2:])
@@ -529,12 +555,14 @@
         functools.partial(score_kernel, members, used, rows, halo),
         (
             chunk(rows + 2 * halo),
-            jax.ShapeDtypeStruct((up(degrees, 128) // 128, share * ens * slots, 128), BF16),
+            pltpu.HBM((up(degrees, 128) // 128, share * ens * slots, 128), BF16),
         ),
         [
             pltpu.VMEM((nlat * share, ens * slots), F32),
             pltpu.VMEM(((nlat + 2 * halo) * share, ens * slots), F32),
             pltpu.VMEM((degrees, degrees), BF16),
+            pltpu.VMEM((up(degrees, 128) // 128, share * ens * slots, 128), BF16),
+            pltpu.SemaphoreType.DMA((share,)),
         ],
         "score",
         work,
@@ -542,6 +570,7 @@
         order_legendre,
         target,
         degree_order.reshape(1, degrees),
+        drained=(1,),
     )
     returned = swap(back)
     packed = call(
@@ -579,10 +608,14 @@
     score_grad = call(
         functools.partial(unpack_kernel, members),
         jax.ShapeDtypeStruct((members, chans, per_owner, 2, orders), F32),
-        [],
+        [
+            pltpu.VMEM((members, chans, per_owner, 2, orders), F32),
+            pltpu.SemaphoreType.DMA((ens_parts, members)),
+        ],
         "unpack",
         work,
         owned,
+        drained=(0,),
     )
     return grad_fields.transpose(0, 2, 1, 3), score_grad.transpose(0, 1, 3, 4, 2)
 

time: 130 us -> 131 us (level); the launches traced: 128 us -> 131 us
  starting transfers between devices: 22.6 us -> 28.2 us
  waiting for transfers between devices: 60.2 us -> 57.4 us
    ppermute x2, starting transfers between devices: 1.53 us -> 6.97 us  [partners(): other = lax.ppermute(outer, 'lat', far)]
    ppermute x2, waiting for transfers between devices: 34.4 us -> 31.6 us  [partners(): one = lax.ppermute(inner, 'lat', near)]
    unnamed x25 -> x23, local copies, waits for them, and re-layouts: 4.04 us -> 2.99 us
where the time goes in v1:
time: 131 us
  waiting for transfers between devices  57.4 us (44%)
  Pallas kernels  36.1 us (28%)
  starting transfers between devices  28.2 us (22%)
  local copies, waits for them, and re-layouts  7.48 us (6%)
    pallas_call x8, Pallas kernels, call(): pl.pallas_call(body, out_shape=outs, in_specs=specs, out_specs=tuple(plac...  36.1 us
    ppermute x2, waiting for transfers between devices, partners(): one = lax.ppermute(inner, 'lat', near)  31.6 us
    all_to_all x3, waiting for transfers between devices, swap(): lax.all_to_all(flat, ('ens', 'lat'), split_axis=0, concat_axis=0, tiled=T...  16.8 us
    all_to_all x3, starting transfers between devices, swap(): lax.all_to_all(flat, ('ens', 'lat'), split_axis=0, concat_axis=0, tiled=T...  12.5 us
    all_to_all x1, waiting for transfers between devices, local(): slab = lax.all_to_all(slab, 'lat', split_axis=0, concat_axis=0, tiled=True)  8.93 us
    ppermute x2, starting transfers between devices, partners(): other = lax.ppermute(outer, 'lat', far)  6.97 us
    ppermute x2, starting transfers between devices, partners(): one = lax.ppermute(inner, 'lat', near)  4.61 us
    all_to_all x1, starting transfers between devices, local(): slab = lax.all_to_all(slab, 'lat', split_axis=0, concat_axis=0, tiled=True)  4.17 us
  transfers between devices with their start and end apart: 8, of which 5 were waited for; matrix products, arithmetic and copies ran while one was open for 2% of the time, Pallas kernels for 18%

profile of v1, /device:TPU:0, one launch (start us, length us, event | category | flops | bytes accessed | tf_op | source)
XLA Modules:
  0.0 130.8 jit_solution(12619872760425921766)
XLA Ops:
  0.7 1.3 dynamic-slice_bitcast_fusion
  1.9 3.1 %collective-permute-start.1 = (bf16[2,3,24,1440]{3,2,1,0:T(8,128)(2,1)S(1)}, bf16[2,3,24,1440]{3,2,1,0:T(8,128)(2,1)S(1)}, u32[]{:S(2)}, u32[]{:S(2)}) collective-permute-start(bf16[2,3,24,1440]{3,2,1,0:T(8,128)(2,1)S(1)} %get-tuple-element.26), channel_id=1, source_target_pairs={{0,1},{1,0},{2,3},{3,2},{4,5},{5,4},{6,7},{7,6},{8,9},{9,8},{10,11... | collective-permute-start | bytes 1244168 | tf_op jit(solution)/shard_map/ppermute | solution.py:37
  5.0 3.5 %collective-permute-start = (bf16[2,3,24,1440]{3,2,1,0:T(8,128)(2,1)S(1)}, bf16[2,3,24,1440]{3,2,1,0:T(8,128)(2,1)S(1)}, u32[]{:S(2)}, u32[]{:S(2)}) collective-permute-start(bf16[2,3,24,1440]{3,2,1,0:T(8,128)(2,1)S(1)} %get-tuple-element.27), channel_id=1, source_target_pairs={{0,7},{1,2},{2,1},{3,4},{4,3},{5,6},{6,5},{7,0},{8,15},{9,10},{10,... | collective-permute-start | bytes 1244168 | tf_op jit(solution)/shard_map/ppermute | solution.py:38
  9.2 6.5 %shard_map.95 = (f32[6,48,1440]{2,1,0:T(8,128)}, bf16[2,96,48]{2,1,0:T(8,128)(2,1)}) custom-call(bf16[2,6,24,1440]{3,2,1,0:T(8,128)(2,1)} %bitcast.35, f32[7,7,24]{2,1,0:T(8,128)} %bitcast.30, bf16[24,24]{1,0:T(8,128)(2,1)} %weight.1, bf16[2,2,96,24]{3,2,1,0:T(8,128)(2,1)} %constant.44.clone.pick), custom_call_target="tpu_custom_call" | custom-call | flops 40642560 | bytes 3317760 | tf_op jit(solution)/shard_map/pallas_call | solution.py:473
  16.3 8.3 %collective-permute-done.1.edge = bf16[2,3,24,1440]{3,2,1,0:T(8,128)(2,1)S(1)} collective-permute-done((bf16[2,3,24,1440]{3,2,1,0:T(8,128)(2,1)S(1)}, bf16[2,3,24,1440]{3,2,1,0:T(8,128)(2,1)S(1)}, u32[]{:S(2)}, u32[]{:S(2)}) %collective-permute-start.1) | collective-permute-done | bytes 414752 | tf_op jit(solution)/shard_map/ppermute | solution.py:37
  25.4 5.3 %shard_map.96 = (bf16[3,96,256]{2,1,0:T(8,128)(2,1)}, bf16[3,48,1440]{2,1,0:T(8,128)(2,1)}) custom-call(s32[2]{0:T(128)} %pad_add_fusion.flags, bf16[2,3,24,1440]{3,2,1,0:T(8,128)(2,1)} %copy-done.10, f32[6,48,1440]{2,1,0:T(8,128)} %get-tuple-element.14.partial, f32[7,7,24]{2,1,0:T(8,128)} %bitcast.31, bf16[1440,512]{1,0:T(8,128)(2,1)} %constant.43.clone.table, ...), custom_call_target="tpu_custom_call" | custom-call | flops 20321280 | bytes 3317760 | tf_op jit(solution)/shard_map/pallas_call | solution.py:473
  31.5 5.6 %shard_map.97 = (bf16[4,8,24,128]{3,2,1,0:T(8,128)(2,1)}, bf16[3,48,1440]{2,1,0:T(8,128)(2,1)}) custom-call(s32[2]{0:T(128)} %pad_add_fusion.flags, bf16[2,3,24,1440]{3,2,1,0:T(8,128)(2,1)} %copy-done.9, f32[6,48,1440]{2,1,0:T(8,128)} %get-tuple-element.14.partial, f32[7,7,24]{2,1,0:T(8,128)} %bitcast.32, bf16[1440,512]{1,0:T(8,128)(2,1)} %constant.43.clone.table, ...), custom_call_target="tpu_custom_call" | custom-call | flops 20321280 | bytes 3317760 | tf_op jit(solution)/shard_map/pallas_call | solution.py:473
  37.1 6.1 %all-to-all-start = ((bf16[32,24,128]{2,1,0:T(8,128)(2,1)}), bf16[32,24,128]{2,1,0:T(8,128)(2,1)S(1)}, u32[]{:S(2)}, u32[]{:S(2)}) async-start(bf16[32,24,128]{2,1,0:T(8,128)(2,1)} %bitcast.40), calls=%async_computation | async-start | bytes 393216 | tf_op jit(solution)/shard_map/all_to_all | solution.py:488
  43.2 0.8 copy.15
  43.9 7.5 %all-to-all-done = bf16[32,24,128]{2,1,0:T(8,128)(2,1)S(1)} async-done(((bf16[32,24,128]{2,1,0:T(8,128)(2,1)}), bf16[32,24,128]{2,1,0:T(8,128)(2,1)S(1)}, u32[]{:S(2)}, u32[]{:S(2)}) %all-to-all-start) | async-done | bytes 196640 | tf_op jit(solution)/shard_map/all_to_all | solution.py:488
  51.4 4.2 %all-to-all-start.1 = ((bf16[8,150,128]{2,1,0:T(8,128)(2,1)}), bf16[8,150,128]{2,1,0:T(8,128)(2,1)S(1)}, u32[]{:S(2)}, u32[]{:S(2)}) async-start(bf16[8,150,128]{2,1,0:T(8,128)(2,1)} %copy.15), calls=%async_computation.1 | async-start | bytes 622592 | tf_op jit(solution)/shard_map/all_to_all | solution.py:535
  55.6 1.0 constant_dynamic-slice_fusion
  56.6 8.9 %all-to-all-done.1 = bf16[8,150,128]{2,1,0:T(8,128)(2,1)S(1)} async-done(((bf16[8,150,128]{2,1,0:T(8,128)(2,1)}), bf16[8,150,128]{2,1,0:T(8,128)(2,1)S(1)}, u32[]{:S(2)}, u32[]{:S(2)}) %all-to-all-start.1) | async-done | bytes 307232 | tf_op jit(solution)/shard_map/all_to_all | solution.py:535
  66.4 5.3 %shard_map.98 = (bf16[4,8,24,256]{3,2,1,0:T(8,128)(2,1)}, bf16[2,2560,128]{2,1,0:T(8,128)(2,1)}) custom-call(bf16[4,8,24,128]{3,2,1,0:T(8,128)(2,1)S(1)} %bitcast.29, bf16[20,48,160]{2,1,0:T(8,128)(2,1)S(1)} %bitcast.27, bf16[20,16,160]{2,1,0:T(8,128)(2,1)S(1)} %pad.4.target, s32[1,160]{1,0:T(1,128)S(1)} %bitcast.34), custom_call_target="tpu_custom_call" | custom-call | flops 40642560 | bytes 3317760 | tf_op jit(solution)/shard_map/pallas_call | solution.py:473
  71.7 3.6 %all-to-all-start.2 = ((bf16[32,24,256]{2,1,0:T(8,128)(2,1)}), bf16[32,24,256]{2,1,0:T(8,128)(2,1)S(1)}, u32[]{:S(2)}, u32[]{:S(2)}) async-start(bf16[32,24,256]{2,1,0:T(8,128)(2,1)} %bitcast.14), calls=%async_computation.2 | async-start | bytes 786432 | tf_op jit(solution)/shard_map/all_to_all | solution.py:488
  75.4 1.4 %copy-done.1 = bf16[2,2560,128]{2,1,0:T(8,128)(2,1)S(1)} copy-done((bf16[2,2560,128]{2,1,0:T(8,128)(2,1)S(1)}, bf16[2,2560,128]{2,1,0:T(8,128)(2,1)}, u32[]{:S(2)}) %copy-start.1) | copy-done | bytes 1310744
  76.8 2.7 %shard_map.101 = bf16[4,8,40,256]{3,2,1,0:T(8,128)(2,1)} custom-call(bf16[2,2560,128]{2,1,0:T(8,128)(2,1)S(1)} %copy-done.1), custom_call_target="tpu_custom_call" | custom-call | flops 40642560 | bytes 3317760 | tf_op jit(solution)/shard_map/pallas_call | solution.py:473
  79.5 9.3 %all-to-all-done.2 = bf16[32,24,256]{2,1,0:T(8,128)(2,1)S(1)} async-done(((bf16[32,24,256]{2,1,0:T(8,128)(2,1)}), bf16[32,24,256]{2,1,0:T(8,128)(2,1)S(1)}, u32[]{:S(2)}, u32[]{:S(2)}) %all-to-all-start.2) | async-done | bytes 393248 | tf_op jit(solution)/shard_map/all_to_all | solution.py:488
  88.8 2.8 %all-to-all-start.3 = ((bf16[32,40,256]{2,1,0:T(8,128)(2,1)}), bf16[32,40,256]{2,1,0:T(8,128)(2,1)S(1)}, u32[]{:S(2)}, u32[]{:S(2)}) async-start(bf16[32,40,256]{2,1,0:T(8,128)(2,1)} %bitcast.17), calls=%async_computation.3 | async-start | bytes 1310720 | tf_op jit(solution)/shard_map/all_to_all | solution.py:488
  91.6 1.5 %collective-permute-start.2 = (bf16[3,48,1440]{2,1,0:T(8,128)(2,1)S(1)}, bf16[3,48,1440]{2,1,0:T(8,128)(2,1)S(1)}, u32[]{:S(2)}, u32[]{:S(2)}) collective-permute-start(bf16[3,48,1440]{2,1,0:T(8,128)(2,1)S(1)} %copy-done.4), channel_id=1, source_target_pairs={{0,1},{1,0},{2,3},{3,2},{4,5},{5,4},{6,7},{7,6},{8,9},{9,8},{10,11... | collective-permute-start | bytes 1244168 | tf_op jit(solution)/shard_map/ppermute | solution.py:37
  93.2 3.4 %collective-permute-start.3 = (bf16[3,48,1440]{2,1,0:T(8,128)(2,1)S(1)}, bf16[3,48,1440]{2,1,0:T(8,128)(2,1)S(1)}, u32[]{:S(2)}, u32[]{:S(2)}) collective-permute-start(bf16[3,48,1440]{2,1,0:T(8,128)(2,1)S(1)} %copy-done.5), channel_id=1, source_target_pairs={{0,7},{1,2},{2,1},{3,4},{4,3},{5,6},{6,5},{7,0},{8,15},{9,10},{10,... | collective-permute-start | bytes 1244168 | tf_op jit(solution)/shard_map/ppermute | solution.py:38
  96.9 23.3 %collective-permute-done.2.near = bf16[3,48,1440]{2,1,0:T(8,128)(2,1)S(1)} collective-permute-done((bf16[3,48,1440]{2,1,0:T(8,128)(2,1)S(1)}, bf16[3,48,1440]{2,1,0:T(8,128)(2,1)S(1)}, u32[]{:S(2)}, u32[]{:S(2)}) %collective-permute-start.2) | collective-permute-done | bytes 414752 | tf_op jit(solution)/shard_map/ppermute | solution.py:37
  120.2 8.2 %shard_map.100 = bf16[2,6,24,1440]{3,2,1,0:T(8,128)(2,1)} custom-call(s32[2]{0:T(128)S(1)} %copy-done.6, bf16[4,8,24,256]{3,2,1,0:T(8,128)(2,1)S(1)} %bitcast.28, bf16[3,48,1440]{2,1,0:T(8,128)(2,1)S(1)} %collective-permute-done.2.near, bf16[3,48,1440]{2,1,0:T(8,128)(2,1)S(1)} %collective-permute-done.3.far, bf16[3,48,1440]{2,1,0:T(8,128)(2,1)S(1)} %copy-done.4, ...), custom_call_target="tpu_custom_call" | custom-call | flops 40642560 | bytes 3317760 | tf_op jit(solution)/shard_map/pallas_call | solution.py:473
  128.4 2.2 %shard_map.102 = f32[2,24,20,2,160]{4,3,2,1,0:T(2,128)} custom-call(bf16[4,8,40,256]{3,2,1,0:T(8,128)(2,1)S(1)} %bitcast.26), custom_call_target="tpu_custom_call" | custom-call | flops 40642560 | bytes 3317760 | tf_op jit(solution)/shard_map/pallas_call | solution.py:473
  (32 shorter events, 4.0 us)
Async XLA Ops:
  0.6 7.9 %copy-start.8 = (bf16[6,160,160]{2,1,0:T(8,128)(2,1)S(1)}, bf16[6,160,160]{2,1,0:T(8,128)(2,1)}, u32[]{:S(2)}) copy-start(bf16[6,160,160]{2,1,0:T(8,128)(2,1)} %param.11) | copy-start | bytes 921604
  1.9 22.7 %collective-permute-start.1 = (bf16[2,3,24,1440]{3,2,1,0:T(8,128)(2,1)S(1)}, bf16[2,3,24,1440]{3,2,1,0:T(8,128)(2,1)S(1)}, u32[]{:S(2)}, u32[]{:S(2)}) collective-permute-start(bf16[2,3,24,1440]{3,2,1,0:T(8,128)(2,1)S(1)} %get-tuple-element.26), channel_id=1, source_target_pairs={{0,1},{1,0},{2,3},{3,2},{4,5},{5,4},{6,7},{7,6},{8,9},{9,8},{10,11... | collective-permute-start | bytes 1244168 | tf_op jit(solution)/shard_map/ppermute | solution.py:37
  5.0 25.7 %collective-permute-start = (bf16[2,3,24,1440]{3,2,1,0:T(8,128)(2,1)S(1)}, bf16[2,3,24,1440]{3,2,1,0:T(8,128)(2,1)S(1)}, u32[]{:S(2)}, u32[]{:S(2)}) collective-permute-start(bf16[2,3,24,1440]{3,2,1,0:T(8,128)(2,1)S(1)} %get-tuple-element.27), channel_id=1, source_target_pairs={{0,7},{1,2},{2,1},{3,4},{4,3},{5,6},{6,5},{7,0},{8,15},{9,10},{10,... | collective-permute-start | bytes 1244168 | tf_op jit(solution)/shard_map/ppermute | solution.py:38
  24.6 0.8 copy-start.10
  30.7 0.8 copy-start.9
  37.1 14.3 %all-to-all-start = ((bf16[32,24,128]{2,1,0:T(8,128)(2,1)}), bf16[32,24,128]{2,1,0:T(8,128)(2,1)S(1)}, u32[]{:S(2)}, u32[]{:S(2)}) async-start(bf16[32,24,128]{2,1,0:T(8,128)(2,1)} %bitcast.40), calls=%async_computation | async-start | bytes 393216 | tf_op jit(solution)/shard_map/all_to_all | solution.py:488
  43.9 22.4 %copy-start.7 = (s32[160]{0:T(256)S(1)}, s32[160]{0:T(256)}, u32[]{:S(2)}) copy-start(s32[160]{0:T(256)} %param.13) | copy-start | bytes 1924
  51.4 14.2 %all-to-all-start.1 = ((bf16[8,150,128]{2,1,0:T(8,128)(2,1)}), bf16[8,150,128]{2,1,0:T(8,128)(2,1)S(1)}, u32[]{:S(2)}, u32[]{:S(2)}) async-start(bf16[8,150,128]{2,1,0:T(8,128)(2,1)} %copy.15), calls=%async_computation.1 | async-start | bytes 622592 | tf_op jit(solution)/shard_map/all_to_all | solution.py:535
  71.7 19.9 %copy-start.4 = (bf16[3,48,1440]{2,1,0:T(8,128)(2,1)S(1)}, bf16[3,48,1440]{2,1,0:T(8,128)(2,1)}, u32[]{:S(2)}) copy-start(bf16[3,48,1440]{2,1,0:T(8,128)(2,1)} %get-tuple-element.23.inner) | copy-start | bytes 1244164
  71.7 24.9 %copy-start.2 = (f32[24,7,7]{0,2,1:T(8,128)S(1)}, f32[24,7,7]{0,2,1:T(8,128)}, u32[]{:S(2)}) copy-start(f32[24,7,7]{0,2,1:T(8,128)} %param.9) | copy-start | bytes 14116
  71.7 17.1 %all-to-all-start.2 = ((bf16[32,24,256]{2,1,0:T(8,128)(2,1)}), bf16[32,24,256]{2,1,0:T(8,128)(2,1)S(1)}, u32[]{:S(2)}, u32[]{:S(2)}) async-start(bf16[32,24,256]{2,1,0:T(8,128)(2,1)} %bitcast.14), calls=%async_computation.2 | async-start | bytes 786432 | tf_op jit(solution)/shard_map/all_to_all | solution.py:488
  75.4 44.8 %copy-start = (bf16[1440,512]{1,0:T(8,128)(2,1)S(1)}, bf16[1440,512]{1,0:T(8,128)(2,1)}, u32[]{:S(2)}) copy-start(bf16[1440,512]{1,0:T(8,128)(2,1)} %constant.43.clone.table) | copy-start | bytes 4423684
  75.4 1.4 %copy-start.1 = (bf16[2,2560,128]{2,1,0:T(8,128)(2,1)S(1)}, bf16[2,2560,128]{2,1,0:T(8,128)(2,1)}, u32[]{:S(2)}) copy-start(bf16[2,2560,128]{2,1,0:T(8,128)(2,1)} %get-tuple-element.25.rounded) | copy-start | bytes 3932164
  76.8 16.3 %copy-start.5 = (bf16[3,48,1440]{2,1,0:T(8,128)(2,1)S(1)}, bf16[3,48,1440]{2,1,0:T(8,128)(2,1)}, u32[]{:S(2)}) copy-start(bf16[3,48,1440]{2,1,0:T(8,128)(2,1)} %get-tuple-element.24.outer) | copy-start | bytes 1244164
  76.8 43.4 %copy-start.3 = (bf16[2,96,48]{2,1,0:T(8,128)(2,1)S(1)}, bf16[2,96,48]{2,1,0:T(8,128)(2,1)}, u32[]{:S(2)}) copy-start(bf16[2,96,48]{2,1,0:T(8,128)(2,1)} %get-tuple-element.15.mixer) | copy-start | bytes 55300
  76.8 43.4 %copy-start.6 = (s32[2]{0:T(128)S(1)}, s32[2]{0:T(128)}, u32[]{:S(2)}) copy-start(s32[2]{0:T(128)} %pad_add_fusion.flags) | copy-start | bytes 28
  88.8 39.6 %all-to-all-start.3 = ((bf16[32,40,256]{2,1,0:T(8,128)(2,1)}), bf16[32,40,256]{2,1,0:T(8,128)(2,1)S(1)}, u32[]{:S(2)}, u32[]{:S(2)}) async-start(bf16[32,40,256]{2,1,0:T(8,128)(2,1)} %bitcast.17), calls=%async_computation.3 | async-start | bytes 1310720 | tf_op jit(solution)/shard_map/all_to_all | solution.py:488
  91.6 28.6 %collective-permute-start.2 = (bf16[3,48,1440]{2,1,0:T(8,128)(2,1)S(1)}, bf16[3,48,1440]{2,1,0:T(8,128)(2,1)S(1)}, u32[]{:S(2)}, u32[]{:S(2)}) collective-permute-start(bf16[3,48,1440]{2,1,0:T(8,128)(2,1)S(1)} %copy-done.4), channel_id=1, source_target_pairs={{0,1},{1,0},{2,3},{3,2},{4,5},{5,4},{6,7},{7,6},{8,9},{9,8},{10,11... | collective-permute-start | bytes 1244168 | tf_op jit(solution)/shard_map/ppermute | solution.py:37
  93.2 27.0 %collective-permute-start.3 = (bf16[3,48,1440]{2,1,0:T(8,128)(2,1)S(1)}, bf16[3,48,1440]{2,1,0:T(8,128)(2,1)S(1)}, u32[]{:S(2)}, u32[]{:S(2)}) collective-permute-start(bf16[3,48,1440]{2,1,0:T(8,128)(2,1)S(1)} %copy-done.5), channel_id=1, source_target_pairs={{0,7},{1,2},{2,1},{3,4},{4,3},{5,6},{6,5},{7,0},{8,15},{9,10},{10,... | collective-permute-start | bytes 1244168 | tf_op jit(solution)/shard_map/ppermute | solution.py:38

commit v2 on v1

--- a/solution.py
+++ b/solution.py
@@ -123,11 +123,16 @@
         mixer[r] = jnp.concatenate(lines, axis=1).astype(BF16)
 
 
-def finish_rows(lower, present, edge, partial, kernel, table, mixer, slope, padded, act, taps):
+def finish_rows(lower, present, edge, partial, kernel, table, mixer, slope, padded, act, taps, sums, waves, got):
     rows, depth, nlon = partial.shape
     size = kernel.shape[0]
     half = size // 2
     span = table.shape[1] // 2
+    start = jnp.where(lower, 0, rows - half)
+    fetch_sums = pltpu.make_async_copy(partial.at[pl.ds(start, half)], sums, got.at[0])
+    fetch_waves = pltpu.make_async_copy(table, waves, got.at[1])
+    fetch_sums.start()
+    fetch_waves.start()
     spread_taps(kernel, taps, False)
     for row in range(half):
         at = jnp.where(lower, row, half - 1 - row)
@@ -135,6 +140,8 @@
         if present is not None:
             value = jnp.where(present, value, jnp.zeros_like(value))
         fill_row(padded, row, value, half)
+
+    fetch_sums.wait()
 
     @pl.loop(0, depth // TILE)
     def _(ct):
@@ -144,14 +151,15 @@
                 (row, jnp.where(lower, row - j, size - 1 - (row - j))) for row in range(j, half)
             ]
             at = jnp.where(lower, j, half - 1 - j)
-            value = partial[jnp.where(lower, j, rows - 1 - j), pl.ds(c0, TILE), :]
+            value = sums[at, pl.ds(c0, TILE), :]
             value = value + tap_sum(padded, taps, c0, lines, size)[:, :nlon]
             value, grad = gelu_pair(value)
             act[at, pl.ds(c0, TILE), :] = value.astype(BF16)
             slope[at, pl.ds(c0, TILE), :] = grad.astype(BF16)
 
+    fetch_waves.wait()
     flat = act[...].reshape(half * depth, nlon)
-    spectral = jnp.dot(flat, table[...], preferred_element_type=F32).astype(BF16)
+    spectral = jnp.dot(flat, waves[...], preferred_element_type=F32).astype(BF16)
     mixed = []
     for j in range(half):
         line = spectral[j * depth : (j + 1) * depth]
@@ -162,18 +170,18 @@
     return mixed
 
 
-def near_kernel(flags, edge, partial, kernel, table, mixer, mixed, slope, padded, act, taps):
+def near_kernel(flags, edge, partial, kernel, table, mixer, mixed, slope, *scratch):
     lines = finish_rows(
-        flags[0] == 1, None, edge, partial, kernel, table, mixer, slope, padded, act, taps
+        flags[0] == 1, None, edge, partial, kernel, table, mixer, slope, *scratch
     )
     for j, line in enumerate(lines):
         mixed[j] = line.astype(BF16)
 
 
-def far_kernel(share, flags, edge, partial, kernel, table, mixer, nearer, out, slope, padded, act, taps):
+def far_kernel(share, flags, edge, partial, kernel, table, mixer, nearer, out, slope, *scratch):
     owners, groups, height, lanes = out.shape
     lines = finish_rows(
-        flags[0] != 1, flags[1] == 1, edge, partial, kernel, table, mixer, slope, padded, act, taps
+        flags[0] != 1, flags[1] == 1, edge, partial, kernel, table, mixer, slope, *scratch
     )
     lines = [nearer[j].astype(F32) for j in range(nearer.shape[0])] + lines
     for t in range(groups):
@@ -463,13 +471,15 @@
     edge = jax.ShapeDtypeStruct((halo, depth, nlon), BF16)
     taps_out = jax.ShapeDtypeStruct((size * size, depth, 128), BF16)
 
-    def call(body, outs, scratch, name, work, *args, drained=()):
+    def call(body, outs, scratch, name, work, *args, drained=(), fetched=()):
         outs = outs if isinstance(outs, tuple) else (outs,)
         places = [
             pl.BlockSpec(memory_space=pltpu.HBM if i in drained else pltpu.VMEM)
             for i in range(len(outs))
         ]
         specs = [scalars if a is flags else whole for a in args]
+        for i in fetched:
+            specs[i] = pl.BlockSpec(memory_space=pltpu.HBM)
         made = pl.pallas_call(
             body,
             out_shape=outs,
@@ -517,6 +527,9 @@
         pltpu.VMEM((halo, depth, wide), BF16),
         pltpu.VMEM((halo, depth, nlon), BF16),
         pltpu.VMEM(taps_out.shape, BF16),
+        pltpu.VMEM((halo, depth, nlon), F32),
+        pltpu.VMEM(table.shape, BF16),
+        pltpu.SemaphoreType.DMA((2,)),
     ]
     mixed, inner = call(
         near_kernel,
@@ -530,6 +543,7 @@
         kernel,
         table,
         mixer,
+        fetched=(2, 4),
     )
     slab, mixed = lax.optimization_barrier((slab, mixed))
     slab = lax.all_to_all(slab, "lat", split_axis=0, concat_axis=0, tiled=True)
@@ -547,6 +561,7 @@
         table,
         mixer,
         mixed,
+        fetched=(2, 4),
     )
     got = swap(sent)
     got, held = lax.optimization_barrier((got, outer))

time: 131 us -> 131 us (level)
  transfers between devices with their start and end apart: 8 -> 8, of which waited for: 5 -> 5; matrix products, arithmetic and copies ran while one was open for 2% -> 2% of each run, Pallas kernels for 18% -> 17%
where the time goes in v2:
time: 131 us
  waiting for transfers between devices  57.4 us (44%)
  Pallas kernels  35.9 us (27%)
  starting transfers between devices  28.3 us (22%)
  local copies, waits for them, and re-layouts  7.47 us (6%)
    pallas_call x8, Pallas kernels, call(): pl.pallas_call(body, out_shape=outs, in_specs=specs, out_specs=tuple(plac...  35.9 us
    ppermute x2, waiting for transfers between devices, partners(): one = lax.ppermute(inner, 'lat', near)  31.6 us
    all_to_all x3, waiting for transfers between devices, swap(): lax.all_to_all(flat, ('ens', 'lat'), split_axis=0, concat_axis=0, tiled=T...  16.8 us
    all_to_all x3, starting transfers between devices, swap(): lax.all_to_all(flat, ('ens', 'lat'), split_axis=0, concat_axis=0, tiled=T...  12.5 us
    all_to_all x1, waiting for transfers between devices, local(): slab = lax.all_to_all(slab, 'lat', split_axis=0, concat_axis=0, tiled=True)  8.93 us
    ppermute x2, starting transfers between devices, partners(): other = lax.ppermute(outer, 'lat', far)  6.97 us
    ppermute x2, starting transfers between devices, partners(): one = lax.ppermute(inner, 'lat', near)  4.61 us
    all_to_all x1, starting transfers between devices, local(): slab = lax.all_to_all(slab, 'lat', split_axis=0, concat_axis=0, tiled=True)  4.17 us
  transfers between devices with their start and end apart: 8, of which 5 were waited for; matrix products, arithmetic and copies ran while one was open for 2% of the time, Pallas kernels for 17%

profile of v2, /device:TPU:0, one launch (start us, length us, event | category | flops | bytes accessed | tf_op | source)
XLA Modules:
  0.0 130.6 jit_solution(2522347575274104316)
XLA Ops:
  0.7 1.3 dynamic-slice_bitcast_fusion
  1.9 3.1 %collective-permute-start.1 = (bf16[2,3,24,1440]{3,2,1,0:T(8,128)(2,1)S(1)}, bf16[2,3,24,1440]{3,2,1,0:T(8,128)(2,1)S(1)}, u32[]{:S(2)}, u32[]{:S(2)}) collective-permute-start(bf16[2,3,24,1440]{3,2,1,0:T(8,128)(2,1)S(1)} %get-tuple-element.26), channel_id=1, source_target_pairs={{0,1},{1,0},{2,3},{3,2},{4,5},{5,4},{6,7},{7,6},{8,9},{9,8},{10,11... | collective-permute-start | bytes 1244168 | tf_op jit(solution)/shard_map/ppermute | solution.py:37
  5.0 3.5 %collective-permute-start = (bf16[2,3,24,1440]{3,2,1,0:T(8,128)(2,1)S(1)}, bf16[2,3,24,1440]{3,2,1,0:T(8,128)(2,1)S(1)}, u32[]{:S(2)}, u32[]{:S(2)}) collective-permute-start(bf16[2,3,24,1440]{3,2,1,0:T(8,128)(2,1)S(1)} %get-tuple-element.27), channel_id=1, source_target_pairs={{0,7},{1,2},{2,1},{3,4},{4,3},{5,6},{6,5},{7,0},{8,15},{9,10},{10,... | collective-permute-start | bytes 1244168 | tf_op jit(solution)/shard_map/ppermute | solution.py:38
  9.2 6.5 %shard_map.95 = (f32[6,48,1440]{2,1,0:T(8,128)}, bf16[2,96,48]{2,1,0:T(8,128)(2,1)}) custom-call(bf16[2,6,24,1440]{3,2,1,0:T(8,128)(2,1)} %bitcast.35, f32[7,7,24]{2,1,0:T(8,128)} %bitcast.30, bf16[24,24]{1,0:T(8,128)(2,1)} %weight.1, bf16[2,2,96,24]{3,2,1,0:T(8,128)(2,1)} %constant.44.clone.pick), custom_call_target="tpu_custom_call" | custom-call | flops 40642560 | bytes 3317760 | tf_op jit(solution)/shard_map/pallas_call | solution.py:483
  16.3 8.3 %collective-permute-done.1.edge = bf16[2,3,24,1440]{3,2,1,0:T(8,128)(2,1)S(1)} collective-permute-done((bf16[2,3,24,1440]{3,2,1,0:T(8,128)(2,1)S(1)}, bf16[2,3,24,1440]{3,2,1,0:T(8,128)(2,1)S(1)}, u32[]{:S(2)}, u32[]{:S(2)}) %collective-permute-start.1) | collective-permute-done | bytes 414752 | tf_op jit(solution)/shard_map/ppermute | solution.py:37
  25.4 5.2 %shard_map.96 = (bf16[3,96,256]{2,1,0:T(8,128)(2,1)}, bf16[3,48,1440]{2,1,0:T(8,128)(2,1)}) custom-call(s32[2]{0:T(128)} %pad_add_fusion.flags, bf16[2,3,24,1440]{3,2,1,0:T(8,128)(2,1)} %copy-done.10, f32[6,48,1440]{2,1,0:T(8,128)} %get-tuple-element.14.partial, f32[7,7,24]{2,1,0:T(8,128)} %bitcast.31, bf16[1440,512]{1,0:T(8,128)(2,1)} %constant.43.clone.table, ...), custom_call_target="tpu_custom_call" | custom-call | flops 20321280 | bytes 3317760 | tf_op jit(solution)/shard_map/pallas_call | solution.py:483
  31.4 5.5 %shard_map.97 = (bf16[4,8,24,128]{3,2,1,0:T(8,128)(2,1)}, bf16[3,48,1440]{2,1,0:T(8,128)(2,1)}) custom-call(s32[2]{0:T(128)} %pad_add_fusion.flags, bf16[2,3,24,1440]{3,2,1,0:T(8,128)(2,1)} %copy-done.9, f32[6,48,1440]{2,1,0:T(8,128)} %get-tuple-element.14.partial, f32[7,7,24]{2,1,0:T(8,128)} %bitcast.32, bf16[1440,512]{1,0:T(8,128)(2,1)} %constant.43.clone.table, ...), custom_call_target="tpu_custom_call" | custom-call | flops 20321280 | bytes 3317760 | tf_op jit(solution)/shard_map/pallas_call | solution.py:483
  36.9 6.1 %all-to-all-start = ((bf16[32,24,128]{2,1,0:T(8,128)(2,1)}), bf16[32,24,128]{2,1,0:T(8,128)(2,1)S(1)}, u32[]{:S(2)}, u32[]{:S(2)}) async-start(bf16[32,24,128]{2,1,0:T(8,128)(2,1)} %bitcast.40), calls=%async_computation | async-start | bytes 393216 | tf_op jit(solution)/shard_map/all_to_all | solution.py:498
  43.0 0.8 copy.15
  43.8 7.5 %all-to-all-done = bf16[32,24,128]{2,1,0:T(8,128)(2,1)S(1)} async-done(((bf16[32,24,128]{2,1,0:T(8,128)(2,1)}), bf16[32,24,128]{2,1,0:T(8,128)(2,1)S(1)}, u32[]{:S(2)}, u32[]{:S(2)}) %all-to-all-start) | async-done | bytes 196640 | tf_op jit(solution)/shard_map/all_to_all | solution.py:498
  51.2 4.2 %all-to-all-start.1 = ((bf16[8,150,128]{2,1,0:T(8,128)(2,1)}), bf16[8,150,128]{2,1,0:T(8,128)(2,1)S(1)}, u32[]{:S(2)}, u32[]{:S(2)}) async-start(bf16[8,150,128]{2,1,0:T(8,128)(2,1)} %copy.15), calls=%async_computation.1 | async-start | bytes 622592 | tf_op jit(solution)/shard_map/all_to_all | solution.py:549
  55.4 1.0 constant_dynamic-slice_fusion
  56.5 8.9 %all-to-all-done.1 = bf16[8,150,128]{2,1,0:T(8,128)(2,1)S(1)} async-done(((bf16[8,150,128]{2,1,0:T(8,128)(2,1)}), bf16[8,150,128]{2,1,0:T(8,128)(2,1)S(1)}, u32[]{:S(2)}, u32[]{:S(2)}) %all-to-all-start.1) | async-done | bytes 307232 | tf_op jit(solution)/shard_map/all_to_all | solution.py:549
  66.2 5.3 %shard_map.98 = (bf16[4,8,24,256]{3,2,1,0:T(8,128)(2,1)}, bf16[2,2560,128]{2,1,0:T(8,128)(2,1)}) custom-call(bf16[4,8,24,128]{3,2,1,0:T(8,128)(2,1)S(1)} %bitcast.29, bf16[20,48,160]{2,1,0:T(8,128)(2,1)S(1)} %bitcast.27, bf16[20,16,160]{2,1,0:T(8,128)(2,1)S(1)} %pad.4.target, s32[1,160]{1,0:T(1,128)S(1)} %bitcast.34), custom_call_target="tpu_custom_call" | custom-call | flops 40642560 | bytes 3317760 | tf_op jit(solution)/shard_map/pallas_call | solution.py:483
  71.6 3.6 %all-to-all-start.2 = ((bf16[32,24,256]{2,1,0:T(8,128)(2,1)}), bf16[32,24,256]{2,1,0:T(8,128)(2,1)S(1)}, u32[]{:S(2)}, u32[]{:S(2)}) async-start(bf16[32,24,256]{2,1,0:T(8,128)(2,1)} %bitcast.14), calls=%async_computation.2 | async-start | bytes 786432 | tf_op jit(solution)/shard_map/all_to_all | solution.py:498
  75.2 1.4 %copy-done.1 = bf16[2,2560,128]{2,1,0:T(8,128)(2,1)S(1)} copy-done((bf16[2,2560,128]{2,1,0:T(8,128)(2,1)S(1)}, bf16[2,2560,128]{2,1,0:T(8,128)(2,1)}, u32[]{:S(2)}) %copy-start.1) | copy-done | bytes 1310744
  76.7 2.7 %shard_map.101 = bf16[4,8,40,256]{3,2,1,0:T(8,128)(2,1)} custom-call(bf16[2,2560,128]{2,1,0:T(8,128)(2,1)S(1)} %copy-done.1), custom_call_target="tpu_custom_call" | custom-call | flops 40642560 | bytes 3317760 | tf_op jit(solution)/shard_map/pallas_call | solution.py:483
  79.3 9.3 %all-to-all-done.2 = bf16[32,24,256]{2,1,0:T(8,128)(2,1)S(1)} async-done(((bf16[32,24,256]{2,1,0:T(8,128)(2,1)}), bf16[32,24,256]{2,1,0:T(8,128)(2,1)S(1)}, u32[]{:S(2)}, u32[]{:S(2)}) %all-to-all-start.2) | async-done | bytes 393248 | tf_op jit(solution)/shard_map/all_to_all | solution.py:498
  88.6 2.8 %all-to-all-start.3 = ((bf16[32,40,256]{2,1,0:T(8,128)(2,1)}), bf16[32,40,256]{2,1,0:T(8,128)(2,1)S(1)}, u32[]{:S(2)}, u32[]{:S(2)}) async-start(bf16[32,40,256]{2,1,0:T(8,128)(2,1)} %bitcast.17), calls=%async_computation.3 | async-start | bytes 1310720 | tf_op jit(solution)/shard_map/all_to_all | solution.py:498
  91.5 1.5 %collective-permute-start.2 = (bf16[3,48,1440]{2,1,0:T(8,128)(2,1)S(1)}, bf16[3,48,1440]{2,1,0:T(8,128)(2,1)S(1)}, u32[]{:S(2)}, u32[]{:S(2)}) collective-permute-start(bf16[3,48,1440]{2,1,0:T(8,128)(2,1)S(1)} %copy-done.4), channel_id=1, source_target_pairs={{0,1},{1,0},{2,3},{3,2},{4,5},{5,4},{6,7},{7,6},{8,9},{9,8},{10,11... | collective-permute-start | bytes 1244168 | tf_op jit(solution)/shard_map/ppermute | solution.py:37
  93.0 3.4 %collective-permute-start.3 = (bf16[3,48,1440]{2,1,0:T(8,128)(2,1)S(1)}, bf16[3,48,1440]{2,1,0:T(8,128)(2,1)S(1)}, u32[]{:S(2)}, u32[]{:S(2)}) collective-permute-start(bf16[3,48,1440]{2,1,0:T(8,128)(2,1)S(1)} %copy-done.5), channel_id=1, source_target_pairs={{0,7},{1,2},{2,1},{3,4},{4,3},{5,6},{6,5},{7,0},{8,15},{9,10},{10,... | collective-permute-start | bytes 1244168 | tf_op jit(solution)/shard_map/ppermute | solution.py:38
  96.7 23.3 %collective-permute-done.2.near = bf16[3,48,1440]{2,1,0:T(8,128)(2,1)S(1)} collective-permute-done((bf16[3,48,1440]{2,1,0:T(8,128)(2,1)S(1)}, bf16[3,48,1440]{2,1,0:T(8,128)(2,1)S(1)}, u32[]{:S(2)}, u32[]{:S(2)}) %collective-permute-start.2) | collective-permute-done | bytes 414752 | tf_op jit(solution)/shard_map/ppermute | solution.py:37
  120.0 8.2 %shard_map.100 = bf16[2,6,24,1440]{3,2,1,0:T(8,128)(2,1)} custom-call(s32[2]{0:T(128)S(1)} %copy-done.6, bf16[4,8,24,256]{3,2,1,0:T(8,128)(2,1)S(1)} %bitcast.28, bf16[3,48,1440]{2,1,0:T(8,128)(2,1)S(1)} %collective-permute-done.2.near, bf16[3,48,1440]{2,1,0:T(8,128)(2,1)S(1)} %collective-permute-done.3.far, bf16[3,48,1440]{2,1,0:T(8,128)(2,1)S(1)} %copy-done.4, ...), custom_call_target="tpu_custom_call" | custom-call | flops 40642560 | bytes 3317760 | tf_op jit(solution)/shard_map/pallas_call | solution.py:483
  128.2 2.2 %shard_map.102 = f32[2,24,20,2,160]{4,3,2,1,0:T(2,128)} custom-call(bf16[4,8,40,256]{3,2,1,0:T(8,128)(2,1)S(1)} %bitcast.26), custom_call_target="tpu_custom_call" | custom-call | flops 40642560 | bytes 3317760 | tf_op jit(solution)/shard_map/pallas_call | solution.py:483
  (32 shorter events, 4.0 us)
Async XLA Ops:
  0.6 7.9 %copy-start.8 = (bf16[6,160,160]{2,1,0:T(8,128)(2,1)S(1)}, bf16[6,160,160]{2,1,0:T(8,128)(2,1)}, u32[]{:S(2)}) copy-start(bf16[6,160,160]{2,1,0:T(8,128)(2,1)} %param.11) | copy-start | bytes 921604
  1.9 22.7 %collective-permute-start.1 = (bf16[2,3,24,1440]{3,2,1,0:T(8,128)(2,1)S(1)}, bf16[2,3,24,1440]{3,2,1,0:T(8,128)(2,1)S(1)}, u32[]{:S(2)}, u32[]{:S(2)}) collective-permute-start(bf16[2,3,24,1440]{3,2,1,0:T(8,128)(2,1)S(1)} %get-tuple-element.26), channel_id=1, source_target_pairs={{0,1},{1,0},{2,3},{3,2},{4,5},{5,4},{6,7},{7,6},{8,9},{9,8},{10,11... | collective-permute-start | bytes 1244168 | tf_op jit(solution)/shard_map/ppermute | solution.py:37
  5.0 25.7 %collective-permute-start = (bf16[2,3,24,1440]{3,2,1,0:T(8,128)(2,1)S(1)}, bf16[2,3,24,1440]{3,2,1,0:T(8,128)(2,1)S(1)}, u32[]{:S(2)}, u32[]{:S(2)}) collective-permute-start(bf16[2,3,24,1440]{3,2,1,0:T(8,128)(2,1)S(1)} %get-tuple-element.27), channel_id=1, source_target_pairs={{0,7},{1,2},{2,1},{3,4},{4,3},{5,6},{6,5},{7,0},{8,15},{9,10},{10,... | collective-permute-start | bytes 1244168 | tf_op jit(solution)/shard_map/ppermute | solution.py:38
  24.6 0.8 copy-start.10
  30.7 0.8 copy-start.9
  36.9 14.3 %all-to-all-start = ((bf16[32,24,128]{2,1,0:T(8,128)(2,1)}), bf16[32,24,128]{2,1,0:T(8,128)(2,1)S(1)}, u32[]{:S(2)}, u32[]{:S(2)}) async-start(bf16[32,24,128]{2,1,0:T(8,128)(2,1)} %bitcast.40), calls=%async_computation | async-start | bytes 393216 | tf_op jit(solution)/shard_map/all_to_all | solution.py:498
  43.8 22.4 %copy-start.7 = (s32[160]{0:T(256)S(1)}, s32[160]{0:T(256)}, u32[]{:S(2)}) copy-start(s32[160]{0:T(256)} %param.13) | copy-start | bytes 1924
  51.2 14.2 %all-to-all-start.1 = ((bf16[8,150,128]{2,1,0:T(8,128)(2,1)}), bf16[8,150,128]{2,1,0:T(8,128)(2,1)S(1)}, u32[]{:S(2)}, u32[]{:S(2)}) async-start(bf16[8,150,128]{2,1,0:T(8,128)(2,1)} %copy.15), calls=%async_computation.1 | async-start | bytes 622592 | tf_op jit(solution)/shard_map/all_to_all | solution.py:549
  71.6 19.9 %copy-start.4 = (bf16[3,48,1440]{2,1,0:T(8,128)(2,1)S(1)}, bf16[3,48,1440]{2,1,0:T(8,128)(2,1)}, u32[]{:S(2)}) copy-start(bf16[3,48,1440]{2,1,0:T(8,128)(2,1)} %get-tuple-element.23.inner) | copy-start | bytes 1244164
  71.6 24.9 %copy-start.2 = (f32[24,7,7]{0,2,1:T(8,128)S(1)}, f32[24,7,7]{0,2,1:T(8,128)}, u32[]{:S(2)}) copy-start(f32[24,7,7]{0,2,1:T(8,128)} %param.9) | copy-start | bytes 14116
  71.6 17.1 %all-to-all-start.2 = ((bf16[32,24,256]{2,1,0:T(8,128)(2,1)}), bf16[32,24,256]{2,1,0:T(8,128)(2,1)S(1)}, u32[]{:S(2)}, u32[]{:S(2)}) async-start(bf16[32,24,256]{2,1,0:T(8,128)(2,1)} %bitcast.14), calls=%async_computation.2 | async-start | bytes 786432 | tf_op jit(solution)/shard_map/all_to_all | solution.py:498
  75.2 44.8 %copy-start = (bf16[1440,512]{1,0:T(8,128)(2,1)S(1)}, bf16[1440,512]{1,0:T(8,128)(2,1)}, u32[]{:S(2)}) copy-start(bf16[1440,512]{1,0:T(8,128)(2,1)} %constant.43.clone.table) | copy-start | bytes 4423684
  75.2 1.4 %copy-start.1 = (bf16[2,2560,128]{2,1,0:T(8,128)(2,1)S(1)}, bf16[2,2560,128]{2,1,0:T(8,128)(2,1)}, u32[]{:S(2)}) copy-start(bf16[2,2560,128]{2,1,0:T(8,128)(2,1)} %get-tuple-element.25.rounded) | copy-start | bytes 3932164
  76.7 16.3 %copy-start.5 = (bf16[3,48,1440]{2,1,0:T(8,128)(2,1)S(1)}, bf16[3,48,1440]{2,1,0:T(8,128)(2,1)}, u32[]{:S(2)}) copy-start(bf16[3,48,1440]{2,1,0:T(8,128)(2,1)} %get-tuple-element.24.outer) | copy-start | bytes 1244164
  76.7 43.4 %copy-start.3 = (bf16[2,96,48]{2,1,0:T(8,128)(2,1)S(1)}, bf16[2,96,48]{2,1,0:T(8,128)(2,1)}, u32[]{:S(2)}) copy-start(bf16[2,96,48]{2,1,0:T(8,128)(2,1)} %get-tuple-element.15.mixer) | copy-start | bytes 55300
  76.7 43.4 %copy-start.6 = (s32[2]{0:T(128)S(1)}, s32[2]{0:T(128)}, u32[]{:S(2)}) copy-start(s32[2]{0:T(128)} %pad_add_fusion.flags) | copy-start | bytes 28
  88.6 39.6 %all-to-all-start.3 = ((bf16[32,40,256]{2,1,0:T(8,128)(2,1)}), bf16[32,40,256]{2,1,0:T(8,128)(2,1)S(1)}, u32[]{:S(2)}, u32[]{:S(2)}) async-start(bf16[32,40,256]{2,1,0:T(8,128)(2,1)} %bitcast.17), calls=%async_computation.3 | async-start | bytes 1310720 | tf_op jit(solution)/shard_map/all_to_all | solution.py:498
  91.5 28.6 %collective-permute-start.2 = (bf16[3,48,1440]{2,1,0:T(8,128)(2,1)S(1)}, bf16[3,48,1440]{2,1,0:T(8,128)(2,1)S(1)}, u32[]{:S(2)}, u32[]{:S(2)}) collective-permute-start(bf16[3,48,1440]{2,1,0:T(8,128)(2,1)S(1)} %copy-done.4), channel_id=1, source_target_pairs={{0,1},{1,0},{2,3},{3,2},{4,5},{5,4},{6,7},{7,6},{8,9},{9,8},{10,11... | collective-permute-start | bytes 1244168 | tf_op jit(solution)/shard_map/ppermute | solution.py:37
  93.0 27.0 %collective-permute-start.3 = (bf16[3,48,1440]{2,1,0:T(8,128)(2,1)S(1)}, bf16[3,48,1440]{2,1,0:T(8,128)(2,1)S(1)}, u32[]{:S(2)}, u32[]{:S(2)}) collective-permute-start(bf16[3,48,1440]{2,1,0:T(8,128)(2,1)S(1)} %copy-done.5), channel_id=1, source_target_pairs={{0,7},{1,2},{2,1},{3,4},{4,3},{5,6},{6,5},{7,0},{8,15},{9,10},{10,... | collective-permute-start | bytes 1244168 | tf_op jit(solution)/shard_map/ppermute | solution.py:38
